TPU v7x, 256 devices: a whole 4x4x8 slice. The times are simulated.
256 devices in a mesh: tm: 32 (over x, y, core), space: 8 (over z).
Axes of the slice: x: 4, y: 4, z: 8, core: 2. Of those that a mesh axis runs over, the one named last changes fastest.
Arguments:
- snapshots: bfloat16 [512, 524288], P('tm', 'space'), may hold values from -6 to 6
- block_lists: int32 [8192, 2], P(('tm', 'space')), may hold values from 0 to 8191
- tile_counts: int32 [8192], P(('tm', 'space')), may hold values from 1 to 2
- remap_weights: bfloat16 [8192, 64, 128], P(('tm', 'space')), may hold values from -0.5 to 0.5
- basis: bfloat16 [524288, 1024], P(('tm', 'space')), may hold values from -6 to 6
- variances: float32 [1024], replicated, may hold values from 0.3 to 3
Outputs:
- coeffs: float32 [1024, 512], P('space')
- rotated: bfloat16 [524288, 1024], P(('tm', 'space'))
Inputs may be any that keep to these rules, and one draw needn't show every extreme that they name: `block_lists`: slots at or beyond a tile's count carry no weight.
All inputs are finite; a program needn't handle non-finite values.
Results may differ from a plain program's by a relative error of at most 0.0043.
Values may be sent and summed in bfloat16 or wider, within the bound.
No kernel may reach another device: no remote copies, remote signals or barrier semaphores. Data moves between devices by JAX's collectives and lax.ppermute only.
A program may use at most 192 MiB of HBM per device.

v0:
```python
import math
import jax
import jax.numpy as jnp
from jax import lax
from jax.sharding import PartitionSpec as P

TILE = 64
MAXB = 2


def per_device(snapshots, block_lists, tile_counts, remap_weights, basis, variances):
    local_tiles = block_lists.shape[0]
    time_rows = snapshots.shape[0]
    tm_size = lax.axis_size("tm")
    list_column, count_column = (
        lax.all_gather(block_lists, "tm", axis=0, tiled=True),
        lax.all_gather(tile_counts, "tm", axis=0, tiled=True),
    )
    gathered = lax.all_gather(snapshots, "space", axis=1, tiled=True)
    cell_total = gathered.shape[1]
    blocks = gathered.reshape(time_rows, cell_total // TILE, TILE)
    picked = blocks[:, list_column.reshape(-1), :].reshape(
        time_rows, tm_size * local_tiles, MAXB * TILE
    )
    slot_index = jnp.arange(MAXB * TILE, dtype=jnp.int32) // TILE
    weight_column = lax.all_gather(remap_weights, "tm", axis=0, tiled=True)
    keep = slot_index[None, :] < count_column[:, None]
    masked = jnp.where(keep[:, None, :], weight_column, jnp.zeros_like(weight_column))
    remap_part = jnp.einsum("kip,tkp->kit", masked, picked, preferred_element_type=jnp.float32)
    remap_part = remap_part.astype(jnp.bfloat16).reshape(tm_size, local_tiles * TILE, time_rows)
    arrived = lax.all_to_all(remap_part, "tm", split_axis=0, concat_axis=2, tiled=True)
    remapped = arrived.reshape(local_tiles * TILE, tm_size * time_rows)
    snap_total = remapped.shape[1]
    partial_coeffs = lax.dot_general(
        basis, remapped, (((0,), (0,)), ((), ())), preferred_element_type=jnp.float32
    )
    coeffs = lax.psum(partial_coeffs, ("tm", "space")) / math.sqrt(cell_total)
    coeff_half = coeffs.astype(jnp.bfloat16)
    coeff_rows = coeffs.shape[0] // lax.axis_size("space")
    own_coeffs = lax.dynamic_slice_in_dim(
        coeffs, lax.axis_index("space") * coeff_rows, coeff_rows, 0
    )
    update = lax.dot_general(
        remapped, coeff_half, (((1,), (1,)), ((), ())), preferred_element_type=jnp.float32
    ) / math.sqrt(snap_total)
    rotated = (basis.astype(jnp.float32) * variances[None, :] + update).astype(jnp.bfloat16)
    return (own_coeffs, rotated)


def solution(mesh):
    return jax.shard_map(
        per_device,
        mesh=mesh,
        in_specs=(
            P("tm", "space"),
            P(("tm", "space"), None),
            P(("tm", "space")),
            P(("tm", "space"), None, None),
            P(("tm", "space"), None),
            P(),
        ),
        out_specs=(P("space", None), P(("tm", "space"), None)),
        check_vma=False,
    )
```

profile of v0, /device:TPU:2, one launch (start us, length us, event | category | flops | bytes accessed | tf_op | source)
XLA Modules:
  0.0 671.5 jit_solution(16009837492111305055)
XLA Ops:
  7.2 0.0 all-gather.6.cloned.1.call-start
  7.2 0.7 all-gather.6.cloned.1.call-update
  7.9 0.0 all-gather.4.cloned.1.call-start
  7.9 0.7 all-gather.4.cloned.1.call-update
  8.6 0.0 all-reduce.3.cloned.1.call-start
  8.7 24.3 %all-gather = s32[32,32,2]{1,2,0:T(2,128)S(1)} all-gather(s32[1,32,2]{1,2,0:T(2,128)} %bitcast.20), channel_id=1, replica_groups=mesh['tm'=32,'space'=8] {'tm'}, dimensions={0}, use_global_device_ids=true | all-gather | bytes 8448 | tf_op jit(solution)/shard_map/all_gather | solution.py:16
  33.0 0.3 copy.16
  33.2 0.3 reshape.86
  33.6 1.3 dynamic-slice
  35.5 0.9 dynamic-update-slice
  36.3 13.8 %all-reduce = s32[1024]{0:T(1024)S(1)} all-reduce(s32[1024]{0:T(1024)S(1)} %dynamic-update-slice), channel_id=1, replica_groups=mesh['tm'=32,'space'=8] {'tm'}, use_global_device_ids=true, to_apply=%add | all-reduce | flops 1024 | bytes 8192
  50.1 0.2 broadcast_compare_fusion
  50.4 135.1 %all-gather.6.cloned.1.call-done = bf16[16,524288]{1,0:T(8,128)(2,1)} async-done(((bf16[16,65536]{1,0:T(8,128)(2,1)}), bf16[16,524288]{1,0:T(8,128)(2,1)}) %all-gather.6.cloned.1.call-update) | async-done | bytes 16777232 | tf_op jit(solution)/shard_map/all_gather | solution.py:19
  185.5 60.5 %reshape.85 = bf16[16,8192,64]{2,1,0:T(8,128)(2,1)} reshape(bf16[16,524288]{1,0:T(8,128)(2,1)} %all-gather.6.cloned.1.call-done) | data formatting | bytes 33554432 | tf_op jit(solution)/shard_map/reshape | solution.py:21
  246.0 29.6 %copy.17 = bf16[16,8192,64]{2,0,1:T(8,128)(2,1)} copy(bf16[16,8192,64]{2,1,0:T(8,128)(2,1)} %reshape.85) | data formatting | bytes 33554432 | tf_op jit(solution)/shard_map/reshape | solution.py:21
  275.6 33.4 %gather_fusion = bf16[2048,16,64]{2,1,0:T(8,128)(2,1)} fusion(bf16[16,8192,64]{2,0,1:T(8,128)(2,1)} %copy.17, s32[2048]{0:T(1024)S(1)} %broadcast_clamp_fusion), kind=kCustom, calls=%fused_computation | custom fusion | bytes 8396800 | tf_op jit(solution)/shard_map/gather | solution.py:22
  309.0 8.8 %copy.18 = bf16[16,2048,64]{2,1,0:T(8,128)(2,1)} copy(bf16[16,2048,64]{2,0,1:T(8,128)(2,1)} %bitcast.16) | data formatting | bytes 8388608 | tf_op jit(solution)/shard_map/gather | solution.py:22
  317.8 11.3 %reshape.87 = bf16[16,1024,128]{2,1,0:T(8,128)(2,1)} reshape(bf16[16,2048,64]{2,1,0:T(8,128)(2,1)} %copy.18) | data formatting | bytes 8388608 | tf_op jit(solution)/shard_map/reshape | solution.py:22
  329.1 0.0 all-gather.4.cloned.1.call-done
  329.1 14.3 %fusion.5 = bf16[1024,64,16]{1,2,0:T(8,128)(2,1)} fusion(bf16[16,1024,128]{2,1,0:T(8,128)(2,1)} %reshape.87, bf16[1024,64,128]{2,1,0:T(8,128)(2,1)} %all-gather.4.cloned.1.call-done, pred[1024,128]{1,0:T(8,128)(4,1)S(1)} %broadcast_compare_fusion), kind=kOutput, calls=%fused_computation.7 | convolution fusion | flops 277872640 | bytes 23199744 | tf_op jit(solution)/shard_map/kip,tkp->kit/dot_general | solution.py:29
  343.3 5.3 copy.20
  348.6 5.8 reshape.88
  354.4 0.0 copy-start
  354.4 1.2 copy.21
  355.5 32.6 %all_to_all.15 = bf16[32,2048,16]{1,2,0:T(8,128)(2,1)S(1)} all-to-all(bf16[32,2048,16]{1,2,0:T(8,128)(2,1)S(1)} %copy.21), channel_id=1, replica_groups=mesh['tm'=32,'space'=8] {'tm'}, dimensions={0} | all-to-all | bytes 4194304 | tf_op jit(solution)/shard_map/all_to_all | solution.py:31
  388.2 0.0 copy-done
  388.2 3.7 convolution_bitcast_fusion
  391.9 0.0 copy-start.1
  391.9 0.0 all-reduce.3.cloned.1.call-update
  391.9 262.6 %all-reduce.3.cloned.1.call-done = f32[1024,512]{0,1:T(8,128)} async-done(((f32[1024,512]{0,1:T(8,128)}), f32[1024,512]{0,1:T(8,128)}) %all-reduce.3.cloned.1.call-update) | async-done | bytes 2097168 | tf_op jit(solution)/shard_map/psum | solution.py:37
  654.6 1.8 broadcast_multiply_fusion
  656.4 0.8 copy.22
  657.3 0.0 copy-done.1
  657.3 7.7 %add_convert_fusion = bf16[2048,1024]{1,0:T(8,128)(2,1)} fusion(bf16[2048,1024]{1,0:T(8,128)(2,1)} %param.10, bf16[2048,512]{0,1:T(8,128)(2,1)S(1)} %bitcast.18, f32[1024]{0:T(1024)S(1)} %copy-done.1, f32[1024,512]{0,1:T(8,128)} %all-reduce.3.cloned.1.call-done), kind=kOutput, calls=%fused_computation.4 | convolution fusion | flops 2159017984 | bytes 12587008 | tf_op jit(solution)/shard_map/dot_general | solution.py:43
  (5 shorter events, 0.1 us)
Async XLA Ops:
  7.2 178.3 %all-gather.6.cloned.1.call-start = ((), (), s32[]{:S(2)}) async-start(), calls=%async_computation.2 | async-start | bytes 18874368 | tf_op jit(solution)/shard_map/all_gather | solution.py:19
  7.9 321.2 %all-gather.4.cloned.1.call-start = ((), (), s32[]{:S(2)}) async-start(), calls=%async_computation.1 | async-start | bytes 17301504 | tf_op jit(solution)/shard_map/all_gather | solution.py:26
  8.6 645.9 %all-reduce.3.cloned.1.call-start = ((), (), s32[]{:S(2)}) async-start(), calls=%async_computation.3 | async-start | bytes 4194304 | tf_op jit(solution)/shard_map/psum | solution.py:37
  354.4 33.8 %copy-start = (bf16[2048,1024]{1,0:T(8,128)(2,1)S(1)}, bf16[2048,1024]{1,0:T(8,128)(2,1)}, u32[]{:S(2)}) copy-start(bf16[2048,1024]{1,0:T(8,128)(2,1)} %param.10) | copy-start | bytes 12582916
  391.9 265.4 %copy-start.1 = (f32[1024]{0:T(1024)S(1)}, f32[1024]{0:T(1024)}, u32[]{:S(2)}) copy-start(f32[1024]{0:T(1024)} %param.11) | copy-start | bytes 12292
Sparse Core Ops, SparseCore 0:
  9.8 175.6 all-gather.5
  188.0 76.1 all-gather.3
  392.0 262.4 all-reduce.2
where the time goes:
time: 673 us; the launch traced here: 671 us
  waiting for transfers between devices  399 us (59%)
  local copies, waits for them, and re-layouts  159 us (24%)
  blocking collectives  70.7 us (11%)
  matrix products  25.6 us (4%)
  between operations  14.5 us (2%)
    psum x1, waiting for transfers between devices, per_device(): coeffs = lax.psum(partial_coeffs, ('tm', 'space')) / math.sqrt(cell_total)  263 us
    all_gather x1, waiting for transfers between devices, per_device(): gathered = lax.all_gather(snapshots, 'space', axis=1, tiled=True)  135 us
    reshape x2, local copies, waits for them, and re-layouts, per_device(): blocks = gathered.reshape(time_rows, cell_total // TILE, TILE)  90.1 us
    gather x2, local copies, waits for them, and re-layouts, per_device(): blocks[:, list_column.reshape(-1), :]  42.2 us
    all_to_all x1, blocking collectives, per_device(): lax.all_to_all(remap_part, 'tm', split_axis=0, concat_axis=2, tiled=True)  32.6 us
    all_gather x1, blocking collectives, per_device(): lax.all_gather(block_lists, 'tm', axis=0, tiled=True)  24.3 us
    dot_general x1, matrix products, per_device(): jnp.einsum('kip,tkp->kit', masked, picked, preferred_element_type=jnp.flo...  14.3 us
    unnamed x1, blocking collectives  13.8 us
  transfers between devices with their start and end apart: 3, of which 2 were waited for; matrix products, arithmetic and copies ran while one was open for 22% of the time, Pallas kernels for 0%

commit v1 on v0

--- a/solution.py
+++ b/solution.py
@@ -34,7 +34,9 @@
     partial_coeffs = lax.dot_general(
         basis, remapped, (((0,), (0,)), ((), ())), preferred_element_type=jnp.float32
     )
-    coeffs = lax.psum(partial_coeffs, ("tm", "space")) / math.sqrt(cell_total)
+    coeffs = lax.psum(lax.psum(partial_coeffs, axis_name="tm"), axis_name="space") / math.sqrt(
+        cell_total
+    )
     coeff_half = coeffs.astype(jnp.bfloat16)
     coeff_rows = coeffs.shape[0] // lax.axis_size("space")
     own_coeffs = lax.dynamic_slice_in_dim(

time: 673 us -> 611 us (0.908)
  waiting for transfers between devices: 399 us -> 337 us
    psum x1 -> x2, waiting for transfers between devices: 263 us -> 200 us  [the longest x1 116 us: per_device(): lax.psum(partial_coeffs, axis_name='tm')]
  transfers between devices with their start and end apart: 3 -> 4, of which waited for: 2 -> 3; matrix products, arithmetic and copies ran while one was open for 22% -> 24% of each run, Pallas kernels for 0% -> 0%
where the time goes in v1:
time: 611 us; the launch traced here: 610 us
  waiting for transfers between devices  337 us (55%)
  local copies, waits for them, and re-layouts  159 us (26%)
  blocking collectives  70.7 us (12%)
  matrix products  25.6 us (4%)
  between operations  14.5 us (2%)
    all_gather x1, waiting for transfers between devices, per_device(): gathered = lax.all_gather(snapshots, 'space', axis=1, tiled=True)  135 us
    psum x1, waiting for transfers between devices, per_device(): lax.psum(partial_coeffs, axis_name='tm')  116 us
    reshape x2, local copies, waits for them, and re-layouts, per_device(): blocks = gathered.reshape(time_rows, cell_total // TILE, TILE)  90.1 us
    psum x1, waiting for transfers between devices, per_device(): lax.psum(lax.psum(partial_coeffs, axis_name='tm'), axis_name='space')  84.8 us
    gather x2, local copies, waits for them, and re-layouts, per_device(): blocks[:, list_column.reshape(-1), :]  42.2 us
    all_to_all x1, blocking collectives, per_device(): lax.all_to_all(remap_part, 'tm', split_axis=0, concat_axis=2, tiled=True)  32.6 us
    all_gather x1, blocking collectives, per_device(): lax.all_gather(block_lists, 'tm', axis=0, tiled=True)  24.3 us
    dot_general x1, matrix products, per_device(): jnp.einsum('kip,tkp->kit', masked, picked, preferred_element_type=jnp.flo...  14.3 us
  transfers between devices with their start and end apart: 4, of which 3 were waited for; matrix products, arithmetic and copies ran while one was open for 24% of the time, Pallas kernels for 0%

profile of v1, /device:TPU:2, one launch (start us, length us, event | category | flops | bytes accessed | tf_op | source)
XLA Modules:
  0.0 609.5 jit_solution(7110356160714147768)
XLA Ops:
  7.2 0.0 all-gather.6.cloned.1.call-start
  7.2 0.7 all-gather.6.cloned.1.call-update
  7.9 0.0 all-gather.4.cloned.1.call-start
  7.9 0.7 all-gather.4.cloned.1.call-update
  8.6 0.0 all-reduce.4.cloned.1.call-start
  8.7 24.3 %all-gather = s32[32,32,2]{1,2,0:T(2,128)S(1)} all-gather(s32[1,32,2]{1,2,0:T(2,128)} %bitcast.20), channel_id=1, replica_groups=mesh['tm'=32,'space'=8] {'tm'}, dimensions={0}, use_global_device_ids=true | all-gather | bytes 8448 | tf_op jit(solution)/shard_map/all_gather | solution.py:16
  33.0 0.3 copy.16
  33.2 0.3 reshape.86
  33.6 1.3 dynamic-slice
  35.5 0.9 dynamic-update-slice
  36.3 13.8 %all-reduce = s32[1024]{0:T(1024)S(1)} all-reduce(s32[1024]{0:T(1024)S(1)} %dynamic-update-slice), channel_id=1, replica_groups=mesh['tm'=32,'space'=8] {'tm'}, use_global_device_ids=true, to_apply=%add | all-reduce | flops 1024 | bytes 8192
  50.1 0.2 broadcast_compare_fusion
  50.4 135.1 %all-gather.6.cloned.1.call-done = bf16[16,524288]{1,0:T(8,128)(2,1)} async-done(((bf16[16,65536]{1,0:T(8,128)(2,1)}), bf16[16,524288]{1,0:T(8,128)(2,1)}) %all-gather.6.cloned.1.call-update) | async-done | bytes 16777232 | tf_op jit(solution)/shard_map/all_gather | solution.py:19
  185.5 60.5 %reshape.85 = bf16[16,8192,64]{2,1,0:T(8,128)(2,1)} reshape(bf16[16,524288]{1,0:T(8,128)(2,1)} %all-gather.6.cloned.1.call-done) | data formatting | bytes 33554432 | tf_op jit(solution)/shard_map/reshape | solution.py:21
  246.0 29.6 %copy.17 = bf16[16,8192,64]{2,0,1:T(8,128)(2,1)} copy(bf16[16,8192,64]{2,1,0:T(8,128)(2,1)} %reshape.85) | data formatting | bytes 33554432 | tf_op jit(solution)/shard_map/reshape | solution.py:21
  275.6 33.4 %gather_fusion = bf16[2048,16,64]{2,1,0:T(8,128)(2,1)} fusion(bf16[16,8192,64]{2,0,1:T(8,128)(2,1)} %copy.17, s32[2048]{0:T(1024)S(1)} %broadcast_clamp_fusion), kind=kCustom, calls=%fused_computation | custom fusion | bytes 8396800 | tf_op jit(solution)/shard_map/gather | solution.py:22
  309.0 8.8 %copy.18 = bf16[16,2048,64]{2,1,0:T(8,128)(2,1)} copy(bf16[16,2048,64]{2,0,1:T(8,128)(2,1)} %bitcast.16) | data formatting | bytes 8388608 | tf_op jit(solution)/shard_map/gather | solution.py:22
  317.8 11.3 %reshape.87 = bf16[16,1024,128]{2,1,0:T(8,128)(2,1)} reshape(bf16[16,2048,64]{2,1,0:T(8,128)(2,1)} %copy.18) | data formatting | bytes 8388608 | tf_op jit(solution)/shard_map/reshape | solution.py:22
  329.1 0.0 all-gather.4.cloned.1.call-done
  329.1 14.3 %fusion.5 = bf16[1024,64,16]{1,2,0:T(8,128)(2,1)} fusion(bf16[16,1024,128]{2,1,0:T(8,128)(2,1)} %reshape.87, bf16[1024,64,128]{2,1,0:T(8,128)(2,1)} %all-gather.4.cloned.1.call-done, pred[1024,128]{1,0:T(8,128)(4,1)S(1)} %broadcast_compare_fusion), kind=kOutput, calls=%fused_computation.7 | convolution fusion | flops 277872640 | bytes 23199744 | tf_op jit(solution)/shard_map/kip,tkp->kit/dot_general | solution.py:29
  343.3 5.3 copy.20
  348.6 5.8 reshape.88
  354.4 0.0 copy-start
  354.4 1.2 copy.21
  355.5 32.6 %all_to_all.15 = bf16[32,2048,16]{1,2,0:T(8,128)(2,1)S(1)} all-to-all(bf16[32,2048,16]{1,2,0:T(8,128)(2,1)S(1)} %copy.21), channel_id=1, replica_groups=mesh['tm'=32,'space'=8] {'tm'}, dimensions={0} | all-to-all | bytes 4194304 | tf_op jit(solution)/shard_map/all_to_all | solution.py:31
  388.2 0.0 copy-done
  388.2 3.7 convolution_bitcast_fusion
  391.9 0.0 all-reduce.4.cloned.1.call-update
  391.9 0.0 copy-start.1
  391.9 0.3 all-reduce.6.cloned.1.call-start
  392.2 115.5 %all-reduce.4.cloned.1.call-done = f32[1024,512]{0,1:T(8,128)} async-done(((f32[1024,512]{0,1:T(8,128)}), f32[1024,512]{0,1:T(8,128)}) %all-reduce.4.cloned.1.call-update) | async-done | bytes 2097168 | tf_op jit(solution)/shard_map/psum | solution.py:37
  507.7 0.0 all-reduce.6.cloned.1.call-update
  507.8 84.8 %all-reduce.6.cloned.1.call-done = f32[1024,512]{0,1:T(8,128)} async-done(((f32[1024,512]{0,1:T(8,128)}), f32[1024,512]{0,1:T(8,128)}) %all-reduce.6.cloned.1.call-update) | async-done | bytes 2097168 | tf_op jit(solution)/shard_map/psum | solution.py:37
  592.6 1.8 broadcast_multiply_fusion
  594.5 0.8 copy.22
  595.3 0.0 copy-done.1
  595.3 7.7 %add_convert_fusion = bf16[2048,1024]{1,0:T(8,128)(2,1)} fusion(bf16[2048,1024]{1,0:T(8,128)(2,1)} %param.10, bf16[2048,512]{0,1:T(8,128)(2,1)S(1)} %bitcast.18, f32[1024]{0:T(1024)S(1)} %copy-done.1, f32[1024,512]{0,1:T(8,128)} %all-reduce.6.cloned.1.call-done), kind=kOutput, calls=%fused_computation.4 | convolution fusion | flops 2159017984 | bytes 12587008 | tf_op jit(solution)/shard_map/dot_general | solution.py:45
  (5 shorter events, 0.1 us)
Async XLA Ops:
  7.2 178.3 %all-gather.6.cloned.1.call-start = ((), (), s32[]{:S(2)}) async-start(), calls=%async_computation.2 | async-start | bytes 18874368 | tf_op jit(solution)/shard_map/all_gather | solution.py:19
  7.9 321.2 %all-gather.4.cloned.1.call-start = ((), (), s32[]{:S(2)}) async-start(), calls=%async_computation.1 | async-start | bytes 17301504 | tf_op jit(solution)/shard_map/all_gather | solution.py:26
  8.6 499.1 %all-reduce.4.cloned.1.call-start = ((), (), s32[]{:S(2)}) async-start(), calls=%async_computation.3 | async-start | bytes 4194304 | tf_op jit(solution)/shard_map/psum | solution.py:37
  354.4 33.8 %copy-start = (bf16[2048,1024]{1,0:T(8,128)(2,1)S(1)}, bf16[2048,1024]{1,0:T(8,128)(2,1)}, u32[]{:S(2)}) copy-start(bf16[2048,1024]{1,0:T(8,128)(2,1)} %param.10) | copy-start | bytes 12582916
  391.9 203.4 %copy-start.1 = (f32[1024]{0:T(1024)S(1)}, f32[1024]{0:T(1024)}, u32[]{:S(2)}) copy-start(f32[1024]{0:T(1024)} %param.11) | copy-start | bytes 12292
  391.9 200.7 %all-reduce.6.cloned.1.call-start = ((), (), s32[]{:S(2)}) async-start(), calls=%async_computation.4 | async-start | bytes 4194304 | tf_op jit(solution)/shard_map/psum | solution.py:37
Sparse Core Ops, SparseCore 0:
  9.8 175.6 all-gather.5
  188.0 76.1 all-gather.3
  392.0 115.6 all-reduce.3
  510.0 82.5 all-reduce.5
